TPU v7x, 32 devices: a whole 2x2x4 slice. The times are simulated.
32 devices in a mesh: layer: 8 (over z, y), group: 4 (over x, core).
Axes of the slice: x: 2, y: 2, z: 4, core: 2. Of those that a mesh axis runs over, the one named last changes fastest.
Arguments:
- travelling_layer_entries: float32 [8, 4, 1024, 256], P('layer', 'group'), may hold values from -6 to 6
- arriving_clusters: float32 [4, 8, 1024, 256], P('group'), may hold values from -6 to 6
- travelling_cluster_position: int32 [8, 4], replicated, may hold values from 0 to 1
- arriving_cluster_position: int32 [4, 8], replicated, may hold values from 0 to 1
- adjacency_patches: bfloat16 [8, 48, 128, 128], P('group'), may hold values from -0.21875 to 0.21875
- patch_read_range: int32 [8, 48], P('group'), may hold values from 0 to 63
- patch_write_range: int32 [8, 48], P('group'), may hold values from 0 to 7
- outdated_layer_entries: bfloat16 [8, 8192, 256], P('layer'), may hold values from -6 to 6
- neighbour_mixing_matrix: bfloat16 [8, 256, 256], P('layer'), may hold values from -0.375 to 0.375
- rescale_factors: float32 [8, 256], P('layer'), may hold values from 0.5 to 1.5
- expand_matrix: bfloat16 [8, 256, 512], P('layer'), may hold values from -0.375 to 0.375
- contract_matrix: bfloat16 [8, 512, 256], P('layer'), may hold values from -0.25 to 0.25
Outputs:
- outputs: float32 [8, 4, 1024, 256], P('layer', 'group')
- history_out: bfloat16 [8, 8192, 256], P('layer')
Inputs may be any that keep to these rules, and one draw needn't show every extreme that they name: `travelling_cluster_position`: local slot of a group within its stream. `arriving_cluster_position`: local slot of a new group within its stream. `patch_read_range`: row block of a layer's whole history.
All inputs are finite; a program needn't handle non-finite values.
Results may differ from a plain program's by a relative error of at most 0.0095.
Values may be sent and summed in bfloat16 or wider, within the bound.
A program may use at most 128 MiB of HBM per device.

v0:
```python
import jax
import jax.numpy as jnp
from jax import lax
from jax.sharding import PartitionSpec as P


def passed_along(shard, axis, by):
    devices = lax.axis_size(axis)
    pairs = [(i, i + by) for i in range(devices) if 0 <= i + by < devices]
    return lax.ppermute(shard, axis, pairs)


def layer_rows(inputs, aggregated, conv_mat, norm_vec, up_mat, down_mat):
    convolved = jnp.dot(aggregated, conv_mat, preferred_element_type=jnp.float32)
    residual_sum = inputs + jax.nn.relu(convolved)
    scale = lax.rsqrt(jnp.mean(residual_sum * residual_sum, axis=-1, keepdims=True) + 1e-06)
    normed = (residual_sum * scale * norm_vec).astype(jnp.bfloat16)
    hidden = jax.nn.gelu(jnp.dot(normed, up_mat, preferred_element_type=jnp.float32)).astype(
        jnp.bfloat16
    )
    return residual_sum + jnp.dot(hidden, down_mat, preferred_element_type=jnp.float32)


def local(
    travelling_layer_entries,
    arriving_clusters,
    travelling_cluster_position,
    arriving_cluster_position,
    adjacency_patches,
    patch_read_range,
    patch_write_range,
    outdated_layer_entries,
    neighbour_mixing_matrix,
    rescale_factors,
    expand_matrix,
    contract_matrix,
):
    streams = lax.axis_size("group")
    layer_pos = lax.axis_index("layer")
    stream_pos = lax.axis_index("group")
    cluster_entry_range = travelling_layer_entries.shape[2]
    inner_breadth = travelling_layer_entries.shape[3]
    per_stream = adjacency_patches.shape[0]
    tile_rows = adjacency_patches.shape[2]
    beat_count = arriving_clusters.shape[1]
    present_carry = travelling_layer_entries[0, 0]
    history_now = outdated_layer_entries[0]
    conv_mat = neighbour_mixing_matrix[0]
    norm_vec = rescale_factors[0]
    up_mat = expand_matrix[0]
    down_mat = contract_matrix[0]
    block_ids = jnp.arange(cluster_entry_range // tile_rows, dtype=jnp.int32)
    result = present_carry
    for beat_no in range(beat_count):
        anchor_point = layer_pos - beat_no
        first_row_index = jnp.clip(anchor_point, 0, travelling_cluster_position.shape[0] - 1)
        feed_col = jnp.clip(beat_no - 1 - layer_pos, 0, beat_count - 1)
        start_offset = lax.dynamic_index_in_dim(
            travelling_cluster_position, first_row_index, 0, keepdims=False
        )
        from_feed = lax.dynamic_index_in_dim(arriving_cluster_position, feed_col, 1, keepdims=False)
        local_slot = jnp.where(anchor_point >= 0, start_offset, from_feed)
        fresh_rows = lax.all_gather(present_carry.astype(jnp.bfloat16), "group", axis=0, tiled=True)
        for peer_pos in range(streams):
            row_start = (peer_pos * per_stream + local_slot[peer_pos]) * cluster_entry_range
            history_now = lax.dynamic_update_slice(
                history_now,
                fresh_rows[peer_pos * cluster_entry_range : (peer_pos + 1) * cluster_entry_range],
                (row_start, jnp.int32(0)),
            )
        own_slot = lax.dynamic_index_in_dim(local_slot, stream_pos, 0, keepdims=False)
        tile_set = lax.dynamic_index_in_dim(adjacency_patches, own_slot, 0, keepdims=False)
        tile_from = lax.dynamic_index_in_dim(patch_read_range, own_slot, 0, keepdims=False)
        tile_to = lax.dynamic_index_in_dim(patch_write_range, own_slot, 0, keepdims=False)
        blocks = history_now.reshape(-1, tile_rows, inner_breadth)[tile_from]
        products = jnp.einsum("tij,tjd->tid", tile_set, blocks, preferred_element_type=jnp.float32)
        onehot = (tile_to[None, :] == block_ids[:, None]).astype(jnp.float32)
        summed = jnp.einsum("bt,tid->bid", onehot, products, precision=lax.Precision.HIGHEST)
        aggregated = summed.reshape(cluster_entry_range, inner_breadth).astype(jnp.bfloat16)
        final_beat = beat_no == beat_count - 1
        half_rows = cluster_entry_range // 2
        pieces = []
        for half_no in range(2):
            lower = half_no * half_rows
            out_piece = layer_rows(
                present_carry[lower : lower + half_rows],
                aggregated[lower : lower + half_rows],
                conv_mat,
                norm_vec,
                up_mat,
                down_mat,
            )
            if not final_beat:
                out_piece = passed_along(out_piece, "layer", 1)
            pieces.append(out_piece)
        joined = jnp.concatenate(pieces, axis=0)
        if final_beat:
            result = joined
        else:
            present_carry = jnp.where(layer_pos == 0, arriving_clusters[0, beat_no], joined)
    return (result[None, None], history_now[None])


def solution(mesh):
    return jax.shard_map(
        local,
        mesh=mesh,
        in_specs=(
            P("layer", "group", None, None),
            P("group", None, None, None),
            P(),
            P(),
            P("group", None, None, None),
            P("group", None),
            P("group", None),
            P("layer", None, None),
            P("layer", None, None),
            P("layer", None),
            P("layer", None, None),
            P("layer", None, None),
        ),
        out_specs=(P("layer", "group", None, None), P("layer", None, None)),
        check_vma=False,
    )
```

profile of v0, /device:TPU:0, one launch (start us, length us, event | category | flops | bytes accessed | tf_op | source)
XLA Modules:
  0.0 714.2 jit_solution(13908586936988195472)
XLA Ops:
  7.3 4.6 copy.242
  50.9 4.7 gather_fusion
  58.4 5.7 fusion.40
  66.0 3.0 convolution_add_fusion.15
  69.0 5.7 collective-permute-start
  76.8 3.0 convolution_add_fusion.14
  79.9 3.9 collective-permute-start.1
  83.8 6.2 fusion.533
  92.6 4.1 collective-permute-done.1
  96.6 3.0 fusion.532
  102.3 22.2 %all-gather.10.cloned.1.call-done = bf16[4096,256]{0,1:T(8,128)(2,1)} async-done(((bf16[1024,256]{0,1:T(8,128)(2,1)}), bf16[4096,256]{0,1:T(8,128)(2,1)}) %all-gather.10.cloned.1.call-update) | async-done | bytes 2097168 | tf_op jit(solution)/shard_map/all_gather | solution.py:63
  143.1 4.7 gather_fusion.1
  150.6 5.7 fusion.43
  158.2 3.0 convolution_add_fusion.13
  161.2 4.2 collective-permute-start.2
  167.5 3.0 convolution_add_fusion.12
  170.6 3.5 collective-permute-start.3
  177.2 10.5 %collective-permute-done.3 = f32[512,256]{0,1:T(8,128)} collective-permute-done((f32[512,256]{0,1:T(8,128)}, f32[512,256]{0,1:T(8,128)}, u32[]{:S(2)}, u32[]{:S(2)}) %collective-permute-start.3) | collective-permute-done | bytes 524320 | tf_op jit(solution)/shard_map/ppermute | solution.py:10
  193.4 21.0 %all-gather.12.cloned.1.call-done = bf16[4096,256]{0,1:T(8,128)(2,1)} async-done(((bf16[1024,256]{0,1:T(8,128)(2,1)}), bf16[4096,256]{0,1:T(8,128)(2,1)}) %all-gather.12.cloned.1.call-update) | async-done | bytes 2097168 | tf_op jit(solution)/shard_map/all_gather | solution.py:63
  214.4 3.0 fusion.539
  233.1 4.7 gather_fusion.2
  240.7 5.7 fusion.46
  248.2 3.0 convolution_add_fusion.11
  251.2 4.2 collective-permute-start.4
  257.5 3.0 convolution_add_fusion.10
  260.6 3.4 collective-permute-start.5
  267.2 10.5 %collective-permute-done.5 = f32[512,256]{0,1:T(8,128)} collective-permute-done((f32[512,256]{0,1:T(8,128)}, f32[512,256]{0,1:T(8,128)}, u32[]{:S(2)}, u32[]{:S(2)}) %collective-permute-start.5) | collective-permute-done | bytes 524320 | tf_op jit(solution)/shard_map/ppermute | solution.py:10
  277.7 3.0 fusion.530
  283.6 20.9 %all-gather.14.cloned.1.call-done = bf16[4096,256]{0,1:T(8,128)(2,1)} async-done(((bf16[1024,256]{0,1:T(8,128)(2,1)}), bf16[4096,256]{0,1:T(8,128)(2,1)}) %all-gather.14.cloned.1.call-update) | async-done | bytes 2097168 | tf_op jit(solution)/shard_map/all_gather | solution.py:63
  323.0 4.7 gather_fusion.3
  330.6 5.7 fusion.49
  338.1 3.1 convolution_add_fusion.9
  341.2 4.2 collective-permute-start.6
  347.5 3.0 convolution_add_fusion.8
  350.6 3.4 collective-permute-start.7
  357.2 10.5 %collective-permute-done.7 = f32[512,256]{0,1:T(8,128)} collective-permute-done((f32[512,256]{0,1:T(8,128)}, f32[512,256]{0,1:T(8,128)}, u32[]{:S(2)}, u32[]{:S(2)}) %collective-permute-start.7) | collective-permute-done | bytes 524320 | tf_op jit(solution)/shard_map/ppermute | solution.py:10
  373.5 20.8 %all-gather.16.cloned.1.call-done = bf16[4096,256]{0,1:T(8,128)(2,1)} async-done(((bf16[1024,256]{0,1:T(8,128)(2,1)}), bf16[4096,256]{0,1:T(8,128)(2,1)}) %all-gather.16.cloned.1.call-update) | async-done | bytes 2097168 | tf_op jit(solution)/shard_map/all_gather | solution.py:63
  412.9 4.7 gather_fusion.4
  420.4 5.7 fusion.52
  427.4 3.0 convolution_add_fusion.7
  430.4 4.2 collective-permute-start.8
  436.8 3.0 convolution_add_fusion.6
  439.8 3.4 collective-permute-start.9
  446.4 10.5 %collective-permute-done.9 = f32[512,256]{0,1:T(8,128)} collective-permute-done((f32[512,256]{0,1:T(8,128)}, f32[512,256]{0,1:T(8,128)}, u32[]{:S(2)}, u32[]{:S(2)}) %collective-permute-start.9) | collective-permute-done | bytes 524320 | tf_op jit(solution)/shard_map/ppermute | solution.py:10
  462.6 21.0 %all-gather.18.cloned.1.call-done = bf16[4096,256]{0,1:T(8,128)(2,1)} async-done(((bf16[1024,256]{0,1:T(8,128)(2,1)}), bf16[4096,256]{0,1:T(8,128)(2,1)}) %all-gather.18.cloned.1.call-update) | async-done | bytes 2097168 | tf_op jit(solution)/shard_map/all_gather | solution.py:63
  502.1 4.7 gather_fusion.5
  509.6 5.7 fusion.55
  516.6 3.0 convolution_add_fusion.5
  519.6 4.2 collective-permute-start.10
  526.0 3.0 convolution_add_fusion.4
  529.0 3.4 collective-permute-start.11
  535.6 10.5 %collective-permute-done.11 = f32[512,256]{0,1:T(8,128)} collective-permute-done((f32[512,256]{0,1:T(8,128)}, f32[512,256]{0,1:T(8,128)}, u32[]{:S(2)}, u32[]{:S(2)}) %collective-permute-start.11) | collective-permute-done | bytes 524320 | tf_op jit(solution)/shard_map/ppermute | solution.py:10
  551.8 21.0 %all-gather.20.cloned.1.call-done = bf16[4096,256]{0,1:T(8,128)(2,1)} async-done(((bf16[1024,256]{0,1:T(8,128)(2,1)}), bf16[4096,256]{0,1:T(8,128)(2,1)}) %all-gather.20.cloned.1.call-update) | async-done | bytes 2097168 | tf_op jit(solution)/shard_map/all_gather | solution.py:63
  591.3 4.7 gather_fusion.6
  598.8 5.7 fusion.58
  605.8 3.1 convolution_add_fusion.3
  608.8 4.2 collective-permute-start.12
  615.2 3.0 convolution_add_fusion.2
  618.2 3.6 collective-permute-start.13
  624.8 10.5 %collective-permute-done.13 = f32[512,256]{0,1:T(8,128)} collective-permute-done((f32[512,256]{0,1:T(8,128)}, f32[512,256]{0,1:T(8,128)}, u32[]{:S(2)}, u32[]{:S(2)}) %collective-permute-start.13) | collective-permute-done | bytes 524320 | tf_op jit(solution)/shard_map/ppermute | solution.py:10
  640.8 21.2 %all-gather.22.cloned.1.call-done = bf16[4096,256]{0,1:T(8,128)(2,1)} async-done(((bf16[1024,256]{0,1:T(8,128)(2,1)}), bf16[4096,256]{0,1:T(8,128)(2,1)}) %all-gather.22.cloned.1.call-update) | async-done | bytes 2097168 | tf_op jit(solution)/shard_map/all_gather | solution.py:63
  680.5 4.7 gather_fusion.7
  688.0 5.7 fusion.61
  696.1 3.0 convolution_add_fusion.1
  (251 shorter events, 245.8 us)
Async XLA Ops:
  7.2 48.4 %copy-start = (bf16[2,48,128,128]{3,2,1,0:T(8,128)(2,1)S(1)}, bf16[2,48,128,128]{3,2,1,0:T(8,128)(2,1)}, u32[]{:S(2)}) copy-start(bf16[2,48,128,128]{3,2,1,0:T(8,128)(2,1)} %param.16) | copy-start | bytes 9437188
  7.2 5.7 copy-start.11
  7.2 6.0 copy-start.12
  7.2 36.2 %all-gather.24.cloned.1.call-start = ((), (), s32[]{:S(2)}) async-start(), calls=%async_computation.7 | async-start | bytes 2621440 | tf_op jit(solution)/shard_map/all_gather | solution.py:63
  7.2 4.6 copy-start.2
  11.9 30.3 %copy-start.13 = (s32[2,48]{1,0:T(2,128)S(1)}, s32[2,48]{1,0:T(2,128)}, u32[]{:S(2)}) copy-start(s32[2,48]{1,0:T(2,128)} %param.17) | copy-start | bytes 1156
  11.9 30.9 %copy-start.14 = (s32[2,48]{1,0:T(2,128)S(1)}, s32[2,48]{1,0:T(2,128)}, u32[]{:S(2)}) copy-start(s32[2,48]{1,0:T(2,128)} %param.18) | copy-start | bytes 1156
  12.8 111.8 %all-gather.10.cloned.1.call-start = ((), (), s32[]{:S(2)}) async-start(), calls=%async_computation | async-start | bytes 2621440 | tf_op jit(solution)/shard_map/all_gather | solution.py:63
  58.4 5.9 copy-start.1
  58.4 5.9 copy-start.10
  69.0 23.6 %collective-permute-start = (f32[512,256]{0,1:T(8,128)}, f32[512,256]{0,1:T(8,128)}, u32[]{:S(2)}, u32[]{:S(2)}) collective-permute-start(f32[512,256]{0,1:T(8,128)} %convolution_add_fusion.15), channel_id=1, source_target_pairs={{0,4},{4,8},{8,12},{12,16},{16,20},{20,24},{24,28},{1,5},{5,9},{9,... | collective-permute-start | bytes 1572872 | tf_op jit(solution)/shard_map/ppermute | solution.py:10
  79.9 16.8 %collective-permute-start.1 = (f32[512,256]{0,1:T(8,128)}, f32[512,256]{0,1:T(8,128)}, u32[]{:S(2)}, u32[]{:S(2)}) collective-permute-start(f32[512,256]{0,1:T(8,128)} %convolution_add_fusion.14), channel_id=1, source_target_pairs={{0,4},{4,8},{8,12},{12,16},{16,20},{20,24},{24,28},{1,5},{5,9},{9,... | collective-permute-start | bytes 1572872 | tf_op jit(solution)/shard_map/ppermute | solution.py:10
  89.9 12.3 %copy-start.24 = (s32[48]{0:T(128)S(1)}, s32[48]{0:T(128)}, u32[]{:S(2)}) copy-start(s32[48]{0:T(128)} %get-tuple-element.102) | copy-start | bytes 580
  99.6 114.8 %all-gather.12.cloned.1.call-start = ((), (), s32[]{:S(2)}) async-start(), calls=%async_computation.1 | async-start | bytes 2621440 | tf_op jit(solution)/shard_map/all_gather | solution.py:63
  147.7 2.9 copy-start.17
  150.6 5.9 copy-start.3
  161.2 16.0 %collective-permute-start.2 = (f32[512,256]{0,1:T(8,128)}, f32[512,256]{0,1:T(8,128)}, u32[]{:S(2)}, u32[]{:S(2)}) collective-permute-start(f32[512,256]{0,1:T(8,128)} %convolution_add_fusion.13), channel_id=1, source_target_pairs={{0,4},{4,8},{8,12},{12,16},{16,20},{20,24},{24,28},{1,5},{5,9},{9,... | collective-permute-start | bytes 1572872 | tf_op jit(solution)/shard_map/ppermute | solution.py:10
  167.5 25.8 %copy-start.23 = (s32[48]{0:T(128)S(1)}, s32[48]{0:T(128)}, u32[]{:S(2)}) copy-start(s32[48]{0:T(128)} %get-tuple-element.101) | copy-start | bytes 580
  170.6 17.1 %collective-permute-start.3 = (f32[512,256]{0,1:T(8,128)}, f32[512,256]{0,1:T(8,128)}, u32[]{:S(2)}, u32[]{:S(2)}) collective-permute-start(f32[512,256]{0,1:T(8,128)} %convolution_add_fusion.12), channel_id=1, source_target_pairs={{0,4},{4,8},{8,12},{12,16},{16,20},{20,24},{24,28},{1,5},{5,9},{9,... | collective-permute-start | bytes 1572872 | tf_op jit(solution)/shard_map/ppermute | solution.py:10
  190.7 113.8 %all-gather.14.cloned.1.call-start = ((), (), s32[]{:S(2)}) async-start(), calls=%async_computation.2 | async-start | bytes 2621440 | tf_op jit(solution)/shard_map/all_gather | solution.py:63
  237.8 2.9 copy-start.16
  240.6 5.9 copy-start.4
  251.2 16.0 %collective-permute-start.4 = (f32[512,256]{0,1:T(8,128)}, f32[512,256]{0,1:T(8,128)}, u32[]{:S(2)}, u32[]{:S(2)}) collective-permute-start(f32[512,256]{0,1:T(8,128)} %convolution_add_fusion.11), channel_id=1, source_target_pairs={{0,4},{4,8},{8,12},{12,16},{16,20},{20,24},{24,28},{1,5},{5,9},{9,... | collective-permute-start | bytes 1572872 | tf_op jit(solution)/shard_map/ppermute | solution.py:10
  257.5 26.1 %copy-start.22 = (s32[48]{0:T(128)S(1)}, s32[48]{0:T(128)}, u32[]{:S(2)}) copy-start(s32[48]{0:T(128)} %get-tuple-element.100) | copy-start | bytes 580
  260.6 17.1 %collective-permute-start.5 = (f32[512,256]{0,1:T(8,128)}, f32[512,256]{0,1:T(8,128)}, u32[]{:S(2)}, u32[]{:S(2)}) collective-permute-start(f32[512,256]{0,1:T(8,128)} %convolution_add_fusion.10), channel_id=1, source_target_pairs={{0,4},{4,8},{8,12},{12,16},{16,20},{20,24},{24,28},{1,5},{5,9},{9,... | collective-permute-start | bytes 1572872 | tf_op jit(solution)/shard_map/ppermute | solution.py:10
  280.7 113.6 %all-gather.16.cloned.1.call-start = ((), (), s32[]{:S(2)}) async-start(), calls=%async_computation.3 | async-start | bytes 2621440 | tf_op jit(solution)/shard_map/all_gather | solution.py:63
  327.7 2.9 copy-start.15
  330.6 5.9 copy-start.5
  341.2 16.0 %collective-permute-start.6 = (f32[512,256]{0,1:T(8,128)}, f32[512,256]{0,1:T(8,128)}, u32[]{:S(2)}, u32[]{:S(2)}) collective-permute-start(f32[512,256]{0,1:T(8,128)} %convolution_add_fusion.9), channel_id=1, source_target_pairs={{0,4},{4,8},{8,12},{12,16},{16,20},{20,24},{24,28},{1,5},{5,9},{9,... | collective-permute-start | bytes 1572872 | tf_op jit(solution)/shard_map/ppermute | solution.py:10
  347.5 26.0 %copy-start.21 = (s32[48]{0:T(128)S(1)}, s32[48]{0:T(128)}, u32[]{:S(2)}) copy-start(s32[48]{0:T(128)} %get-tuple-element.99) | copy-start | bytes 580
  350.6 17.1 %collective-permute-start.7 = (f32[512,256]{0,1:T(8,128)}, f32[512,256]{0,1:T(8,128)}, u32[]{:S(2)}, u32[]{:S(2)}) collective-permute-start(f32[512,256]{0,1:T(8,128)} %convolution_add_fusion.8), channel_id=1, source_target_pairs={{0,4},{4,8},{8,12},{12,16},{16,20},{20,24},{24,28},{1,5},{5,9},{9,... | collective-permute-start | bytes 1572872 | tf_op jit(solution)/shard_map/ppermute | solution.py:10
  370.6 113.0 %all-gather.18.cloned.1.call-start = ((), (), s32[]{:S(2)}) async-start(), calls=%async_computation.4 | async-start | bytes 2621440 | tf_op jit(solution)/shard_map/all_gather | solution.py:63
  420.4 5.9 copy-start.6
  430.4 16.0 %collective-permute-start.8 = (f32[512,256]{0,1:T(8,128)}, f32[512,256]{0,1:T(8,128)}, u32[]{:S(2)}, u32[]{:S(2)}) collective-permute-start(f32[512,256]{0,1:T(8,128)} %convolution_add_fusion.7), channel_id=1, source_target_pairs={{0,4},{4,8},{8,12},{12,16},{16,20},{20,24},{24,28},{1,5},{5,9},{9,... | collective-permute-start | bytes 1572872 | tf_op jit(solution)/shard_map/ppermute | solution.py:10
  436.8 25.8 %copy-start.20 = (s32[48]{0:T(128)S(1)}, s32[48]{0:T(128)}, u32[]{:S(2)}) copy-start(s32[48]{0:T(128)} %get-tuple-element.98) | copy-start | bytes 580
  439.8 17.1 %collective-permute-start.9 = (f32[512,256]{0,1:T(8,128)}, f32[512,256]{0,1:T(8,128)}, u32[]{:S(2)}, u32[]{:S(2)}) collective-permute-start(f32[512,256]{0,1:T(8,128)} %convolution_add_fusion.6), channel_id=1, source_target_pairs={{0,4},{4,8},{8,12},{12,16},{16,20},{20,24},{24,28},{1,5},{5,9},{9,... | collective-permute-start | bytes 1572872 | tf_op jit(solution)/shard_map/ppermute | solution.py:10
  459.9 112.9 %all-gather.20.cloned.1.call-start = ((), (), s32[]{:S(2)}) async-start(), calls=%async_computation.5 | async-start | bytes 2621440 | tf_op jit(solution)/shard_map/all_gather | solution.py:63
  509.6 5.9 copy-start.7
  509.6 7.0 copy-start.26
  519.6 16.0 %collective-permute-start.10 = (f32[512,256]{0,1:T(8,128)}, f32[512,256]{0,1:T(8,128)}, u32[]{:S(2)}, u32[]{:S(2)}) collective-permute-start(f32[512,256]{0,1:T(8,128)} %convolution_add_fusion.5), channel_id=1, source_target_pairs={{0,4},{4,8},{8,12},{12,16},{16,20},{20,24},{24,28},{1,5},{5,9},{9,... | collective-permute-start | bytes 1572872 | tf_op jit(solution)/shard_map/ppermute | solution.py:10
  526.0 25.8 %copy-start.19 = (s32[48]{0:T(128)S(1)}, s32[48]{0:T(128)}, u32[]{:S(2)}) copy-start(s32[48]{0:T(128)} %get-tuple-element.104) | copy-start | bytes 580
  529.0 17.1 %collective-permute-start.11 = (f32[512,256]{0,1:T(8,128)}, f32[512,256]{0,1:T(8,128)}, u32[]{:S(2)}, u32[]{:S(2)}) collective-permute-start(f32[512,256]{0,1:T(8,128)} %convolution_add_fusion.4), channel_id=1, source_target_pairs={{0,4},{4,8},{8,12},{12,16},{16,20},{20,24},{24,28},{1,5},{5,9},{9,... | collective-permute-start | bytes 1572872 | tf_op jit(solution)/shard_map/ppermute | solution.py:10
  549.1 112.9 %all-gather.22.cloned.1.call-start = ((), (), s32[]{:S(2)}) async-start(), calls=%async_computation.6 | async-start | bytes 2621440 | tf_op jit(solution)/shard_map/all_gather | solution.py:63
  598.8 5.9 copy-start.8
  608.8 16.0 %collective-permute-start.12 = (f32[512,256]{0,1:T(8,128)}, f32[512,256]{0,1:T(8,128)}, u32[]{:S(2)}, u32[]{:S(2)}) collective-permute-start(f32[512,256]{0,1:T(8,128)} %convolution_add_fusion.3), channel_id=1, source_target_pairs={{0,4},{4,8},{8,12},{12,16},{16,20},{20,24},{24,28},{1,5},{5,9},{9,... | collective-permute-start | bytes 1572872 | tf_op jit(solution)/shard_map/ppermute | solution.py:10
  615.2 25.6 %copy-start.18 = (s32[48]{0:T(128)S(1)}, s32[48]{0:T(128)}, u32[]{:S(2)}) copy-start(s32[48]{0:T(128)} %get-tuple-element.97) | copy-start | bytes 580
  618.2 17.1 %collective-permute-start.13 = (f32[512,256]{0,1:T(8,128)}, f32[512,256]{0,1:T(8,128)}, u32[]{:S(2)}, u32[]{:S(2)}) collective-permute-start(f32[512,256]{0,1:T(8,128)} %convolution_add_fusion.2), channel_id=1, source_target_pairs={{0,4},{4,8},{8,12},{12,16},{16,20},{20,24},{24,28},{1,5},{5,9},{9,... | collective-permute-start | bytes 1572872 | tf_op jit(solution)/shard_map/ppermute | solution.py:10
  688.0 5.9 copy-start.9
  693.7 2.4 copy-start.25
Sparse Core Ops, SparseCore 0:
  12.9 25.2 all-gather.23
  99.8 24.7 all-gather.9
  190.8 23.5 all-gather.11
  280.9 23.5 all-gather.13
  370.7 23.5 all-gather.15
  460.0 23.5 all-gather.17
  549.2 23.5 all-gather.19
  638.4 23.5 all-gather.21
where the time goes:
time: 728 us; the launch traced here: 714 us
  local copies, waits for them, and re-layouts  221 us (30%)
  waiting for transfers between devices  219 us (30%)
  matrix products  141 us (19%)
  starting transfers between devices  56.6 us (8%)
  between operations  50 us (7%)
  other arithmetic  26.9 us (4%)
    all_gather x8, waiting for transfers between devices, local(): lax.all_gather(present_carry.astype(jnp.bfloat16), 'group', axis=0, tiled...  148 us
    slice x35, local copies, waits for them, and re-layouts, local(): fresh_rows[peer_pos * cluster_entry_range:(peer_pos + 1) * cluster_entry_...  77.5 us
    ppermute x14, waiting for transfers between devices, passed_along(): return lax.ppermute(shard, axis, pairs)  70.6 us
    dynamic_update_slice x32, local copies, waits for them, and re-layouts, local(): lax.dynamic_update_slice(history_now, fresh_rows[peer_pos * cluster_entry...  59.8 us
    ppermute x14, starting transfers between devices, passed_along(): return lax.ppermute(shard, axis, pairs)  55.3 us
    dot_general x16, matrix products, layer_rows(): jnp.dot(hidden, down_mat, preferred_element_type=jnp.float32)  48.4 us
    dot_general x8, matrix products, local(): jnp.einsum('bt,tid->bid', onehot, products, precision=lax.Precision.HIGHEST)  45.3 us
    gather x8, local copies, waits for them, and re-layouts, local(): blocks = history_now.reshape(-1, tile_rows, inner_breadth)[tile_from]  37.4 us
  transfers between devices with their start and end apart: 22, of which 20 were waited for; matrix products, arithmetic and copies ran while one was open for 10% of the time, Pallas kernels for 0%

commit v1 on v0

v1 whole, which is shorter than its diff:
```python
import functools

import jax
import jax.numpy as jnp
from jax import lax
from jax.experimental import pallas as pl
from jax.experimental.pallas import tpu as pltpu
from jax.sharding import PartitionSpec as P

MESH = pl.DeviceIdType.MESH
CHUNKS = 4
UNROLL = 4


def pair_count(tiles, nb):
    pairs = (tiles + nb) // 2
    return -(-pairs // UNROLL) * UNROLL


def kernel(
    layers, streams, per_stream, beats, rows, tb, pairs,
    a_idx, b_row, keep, last, final_row,
    act_ref, feed_ref, tile_ref, hist_ref, mix_ref, gain_ref, up_ref, down_ref,
    out_ref, hist_out,
    hist, tiles, land, stage, segs, sbuf,
    local_sem, hist_sem, tile_sem, y_send, y_recv, sib_send, sib_recv, x_send, x_recv, r_send, r_recv,
):
    layer = lax.axis_index("layer")
    me = lax.axis_index("group")
    core = lax.rem(me, 2)
    sib = me + 1 - 2 * core
    cross = lax.rem(me + 2, streams)
    cross_sib = cross + 1 - 2 * core
    crows = rows // CHUNKS
    nb = rows // tb
    slots = streams * per_stream
    first_layer = layer == 0
    last_layer = layer == layers - 1

    old = pltpu.make_async_copy(hist_ref, hist.at[pl.ds(0, slots * nb)], hist_sem)
    old.start()
    load = pltpu.make_async_copy(tile_ref, tiles.at[pl.ds(0, tile_ref.shape[0])], tile_sem)
    load.start()
    tiles[tile_ref.shape[0]] = jnp.zeros((tb, tb), jnp.bfloat16)
    segs[pairs] = jnp.zeros((tb, hist.shape[2]), jnp.bfloat16)

    barrier = pltpu.get_barrier_semaphore()
    for peer in (sib, cross):
        pl.semaphore_signal(barrier, inc=1, device_id={"group": peer}, device_id_type=MESH)

    @pl.when(layer > 0)
    def _():
        pl.semaphore_signal(barrier, inc=1, device_id={"layer": layer - 1}, device_id_type=MESH)

    @pl.when(layer < layers - 1)
    def _():
        pl.semaphore_signal(barrier, inc=1, device_id={"layer": layer + 1}, device_id_type=MESH)

    inner = (layer > 0).astype(jnp.int32) + (layer < layers - 1).astype(jnp.int32)
    pl.semaphore_wait(barrier, 2 + inner)

    def piece(k):
        return pl.ds(pl.multiple_of(k * crows, crows), crows)

    def y_copy(b, k):
        return pltpu.make_async_remote_copy(
            src_ref=sbuf.at[piece(k)],
            dst_ref=land.at[b, me, piece(k)],
            send_sem=y_send.at[k],
            recv_sem=y_recv.at[b, k],
            device_id={"layer": layer + 1},
            device_id_type=MESH,
        )

    def group_copy(b, k, stream, send, recv, to):
        return pltpu.make_async_remote_copy(
            src_ref=land.at[b, stream, piece(k)],
            dst_ref=land.at[b, stream, piece(k)],
            send_sem=send.at[k],
            recv_sem=recv.at[b, k],
            device_id={"group": to},
            device_id_type=MESH,
        )

    def keep_rows(b, stream, k):
        at = (slots + b * streams + stream) * nb + k * (crows // tb)
        for u in range(crows // tb):
            hist[at + u] = land[b, stream, pl.ds(k * crows + u * tb, tb), :]

    def beat(b, carry):
        source = jnp.logical_or(b == 0, first_layer)

        @pl.when(b == 0)
        def _():
            c = pltpu.make_async_copy(act_ref, stage, local_sem)
            c.start()
            c.wait()

        @pl.when(jnp.logical_and(b > 0, first_layer))
        def _():
            c = pltpu.make_async_copy(feed_ref.at[jnp.maximum(b - 1, 0)], stage, local_sem)
            c.start()
            c.wait()

        def cross_in(k):
            group_copy(b, k, cross, x_send, x_recv, cross).wait_recv()
            group_copy(b, k, cross, r_send, r_recv, sib).start()
            keep_rows(b, cross, k)

        for k in range(CHUNKS):
            @pl.when(source)
            def _():
                land[b, me, piece(k), :] = stage[piece(k), :].astype(jnp.bfloat16)

            @pl.when(jnp.logical_not(source))
            def _():
                y_copy(b, k).wait_recv()

            group_copy(b, k, me, x_send, x_recv, cross).start()
            group_copy(b, k, me, sib_send, sib_recv, sib).start()
            keep_rows(b, me, k)
            if k > 0:
                cross_in(k - 1)
        for k in range(CHUNKS):
            group_copy(b, k, sib, sib_send, sib_recv, sib).wait_recv()
            keep_rows(b, sib, k)
        cross_in(CHUNKS - 1)
        for k in range(CHUNKS):
            group_copy(b, k, cross_sib, r_send, r_recv, sib).wait_recv()
            keep_rows(b, cross_sib, k)

        @pl.when(b == 0)
        def _():
            old.wait()
            load.wait()

        def one_pair(q, total):
            def half(h):
                i = 2 * q + h
                return tiles[a_idx[b, i]], hist[b_row[b, i]]

            t0, b0 = half(0)
            t1, b1 = half(1)
            product = jnp.dot(
                jnp.concatenate([t0, t1], axis=1),
                jnp.concatenate([b0, b1], axis=0),
                preferred_element_type=jnp.float32,
            )
            total = total * keep[b, q] + product
            segs[q] = total.astype(jnp.bfloat16)
            return total

        def pair_step(s, total):
            for u in range(UNROLL):
                total = one_pair(s * UNROLL + u, total)
            return total

        width = hist.shape[2]
        lax.fori_loop(0, pairs // UNROLL, pair_step, jnp.zeros((tb, width), jnp.float32))

        def rows_step(k):
            blocks = []
            per = crows // tb
            for u in range(per):
                blocks.append(segs[last[b, k * per + u]])
            agg = jnp.concatenate(blocks, axis=0) if per > 1 else blocks[0]
            act = land[b, me, piece(k), :].astype(jnp.float32)
            mixed = act + jnp.maximum(
                jnp.dot(agg, mix_ref[...], preferred_element_type=jnp.float32), 0.0
            )
            scale = lax.rsqrt(jnp.mean(mixed * mixed, axis=-1, keepdims=True) + 1e-06)
            normed = (mixed * scale * gain_ref[...]).astype(jnp.bfloat16)
            hidden = jax.nn.gelu(
                jnp.dot(normed, up_ref[...], preferred_element_type=jnp.float32)
            ).astype(jnp.bfloat16)
            return mixed + jnp.dot(hidden, down_ref[...], preferred_element_type=jnp.float32)

        sends = jnp.logical_and(b < beats - 1, layer < layers - 1)
        for k in range(CHUNKS):
            @pl.when(jnp.logical_and(b > 0, layer < layers - 1))
            def _():
                y_copy(b, k).wait_send()

            res = rows_step(k)
            out_ref[piece(k), :] = res
            sbuf[piece(k), :] = res.astype(jnp.bfloat16)

            @pl.when(sends)
            def _():
                y_copy(b + 1, k).start()

        for k in range(CHUNKS):
            group_copy(b, k, me, x_send, x_recv, cross).wait_send()
            group_copy(b, k, me, sib_send, sib_recv, sib).wait_send()
            group_copy(b, k, cross, r_send, r_recv, sib).wait_send()
        return carry

    lax.fori_loop(0, beats, beat, 0)

    def final(i, carry):
        hist_out[i] = hist[final_row[0, i]]
        return carry

    lax.fori_loop(0, slots * nb, final, 0)


def tables(layer, me, tpos, apos, read, write, rows, tb):
    beats = apos.shape[1]
    streams = apos.shape[0]
    per_stream, tiles = read.shape
    nb = rows // tb
    slots = streams * per_stream
    pairs = pair_count(tiles, nb)
    i32 = jnp.int32
    seq = jnp.concatenate([apos.T[::-1], tpos], axis=0)
    slot = lax.dynamic_slice_in_dim(seq, layer + 1, beats, 0)[::-1]
    own = lax.dynamic_slice_in_dim(slot, me, 1, 1)[:, 0]
    bs = jnp.arange(beats, dtype=i32)
    js = jnp.arange(per_stream, dtype=i32)
    hit = (slot[None, :, :, None] == js) & (bs[None, :, None, None] <= bs[:, None, None, None])
    latest = jnp.max(jnp.where(hit, bs[None, :, None, None], -1), axis=1)
    cs = jnp.arange(streams, dtype=i32)
    cur = jnp.where(
        latest >= 0, slots + streams * latest + cs[None, :, None], cs[None, :, None] * per_stream + js
    ).reshape(beats, slots)
    ks = jnp.arange(nb, dtype=i32)
    ts = jnp.arange(tiles, dtype=i32)
    onto = write[:, :, None] == ks
    count = jnp.sum(onto.astype(i32), axis=1)
    half = (count + 1) // 2
    start = jnp.sum(jnp.where(ks[None, :, None] > ks[None, None, :], half[:, None, :], 0), axis=2)
    rank = jnp.sum(
        ((write[:, :, None] == write[:, None, :]) & (ts[None, None, :] < ts[None, :, None])).astype(i32),
        axis=2,
    )
    place = 2 * jnp.sum(jnp.where(onto, start[:, None, :], 0), axis=2) + rank
    qs = jnp.arange(2 * pairs, dtype=i32)
    at = place[:, None, :] == qs[None, :, None]
    ok = jnp.any(at, axis=2).astype(i32)
    tile = jnp.sum(jnp.where(at, ts, 0), axis=2) + jnp.where(ok > 0, js[:, None] * tiles, per_stream * tiles)
    block = jnp.sum(jnp.where(at, read[:, None, :], 0), axis=2)
    ps = jnp.arange(pairs, dtype=i32)
    resets = jnp.any((ps[None, :, None] == start[:, None, :]) & (half > 0)[:, None, :], axis=2)
    keep = 1.0 - resets.astype(jnp.float32)
    last = jnp.where(half > 0, start + half - 1, pairs)
    mine = own[:, None] == js

    def pick(x):
        return jnp.sum(jnp.where(mine[:, :, None], x[None], 0), axis=1)

    block_b = pick(block)
    ss = jnp.arange(slots, dtype=i32)
    base = jnp.sum(
        jnp.where((block_b // nb)[:, :, None] == ss, cur[:, None, :], 0), axis=2
    )
    b_row = base * nb + block_b % nb
    final_row = (cur[beats - 1][:, None] * nb + ks).reshape(1, slots * nb)
    return pick(tile), b_row, pick(keep), pick(last), final_row


def solution(mesh):
    layers = mesh.shape["layer"]
    streams = mesh.shape["group"]

    def local(act, feed, tpos, apos, tiles, read, write, hist, mix, gain, up, down):
        rows, width = act.shape[2:]
        per_stream, n_tiles, tb = tiles.shape[:3]
        beats = feed.shape[1]
        nb = rows // tb
        slots = streams * per_stream
        pairs = pair_count(n_tiles, nb)
        tabs = tables(
            lax.axis_index("layer"), lax.axis_index("group"), tpos, apos, read, write, rows, tb
        )
        smem = pl.BlockSpec(memory_space=pltpu.SMEM)
        vmem = pl.BlockSpec(memory_space=pltpu.VMEM)
        hbm = pl.BlockSpec(memory_space=pl.ANY)
        dma = pltpu.SemaphoreType.DMA
        out, hist_new = pl.pallas_call(
            functools.partial(kernel, layers, streams, per_stream, beats, rows, tb, pairs),
            out_shape=(
                jax.ShapeDtypeStruct((rows, width), jnp.float32),
                jax.ShapeDtypeStruct((slots * nb, tb, width), jnp.bfloat16),
            ),
            in_specs=[smem] * 5 + [hbm, hbm, hbm, hbm, vmem, vmem, vmem, vmem],
            out_specs=(vmem, vmem),
            scratch_shapes=[
                pltpu.VMEM(((slots + beats * streams) * nb, tb, width), jnp.bfloat16),
                pltpu.VMEM((per_stream * n_tiles + 1, tb, tb), jnp.bfloat16),
                pltpu.VMEM((beats, streams, rows, width), jnp.bfloat16),
                pltpu.VMEM((rows, width), jnp.float32),
                pltpu.VMEM((pairs + 1, tb, width), jnp.bfloat16),
                pltpu.VMEM((rows, width), jnp.bfloat16),
                dma,
                dma,
                dma,
                dma((CHUNKS,)),
                dma((beats, CHUNKS)),
                dma((CHUNKS,)),
                dma((beats, CHUNKS)),
                dma((CHUNKS,)),
                dma((beats, CHUNKS)),
                dma((CHUNKS,)),
                dma((beats, CHUNKS)),
            ],
            compiler_params=pltpu.CompilerParams(
                collective_id=0, has_side_effects=True, vmem_limit_bytes=64000000
            ),
        )(
            *tabs,
            act[0, 0],
            feed[0],
            tiles.reshape(per_stream * n_tiles, tb, tb),
            hist[0].reshape(slots * nb, tb, width),
            mix[0],
            gain,
            up[0],
            down[0],
        )
        return out[None, None], hist_new.reshape(1, slots * rows, width)

    return jax.shard_map(
        local,
        mesh=mesh,
        in_specs=(
            P("layer", "group", None, None),
            P("group", None, None, None),
            P(),
            P(),
            P("group", None, None, None),
            P("group", None),
            P("group", None),
            P("layer", None, None),
            P("layer", None, None),
            P("layer", None),
            P("layer", None, None),
            P("layer", None, None),
        ),
        out_specs=(P("layer", "group", None, None), P("layer", None, None)),
        check_vma=False,
    )
```

time: 728 us -> 193 us (0.27)
  the two profiles are of different devices: /device:TPU:0 before, /device:TPU:31 now
where the time goes in v1:
time: 193 us
  Pallas kernels  175 us (91%)
  local copies, waits for them, and re-layouts  8.86 us (5%)
  other arithmetic  7.93 us (4%)
    pallas_call x1, Pallas kernels, local(): pl.pallas_call(functools.partial(kernel, layers, streams, per_stream, bea...  175 us
    unnamed x2, local copies, waits for them, and re-layouts  6.73 us

profile of v1, /device:TPU:31, one launch (start us, length us, event | category | flops | bytes accessed | tf_op | source)
XLA Modules:
  0.0 192.9 jit_solution(3080644029772010344)
XLA Ops:
  0.7 0.8 convert_reduce_fusion.1
  1.5 0.1 select_reduce_fusion.9
  1.7 0.1 fusion.2
  1.8 0.8 select_reduce_fusion.8
  2.5 0.1 iota_add_fusion.2
  2.6 0.1 add.175
  2.7 0.1 add.176
  2.8 0.8 rev.6
  3.5 0.8 pad_add_fusion
  4.3 0.1 constant_dynamic-slice_fusion
  4.4 0.1 rev.7
  4.5 0.2 select_reduce_fusion.3
  4.7 0.2 fusion.5
  5.0 0.1 mul.62
  5.1 0.1 add.178
  5.2 0.1 add.172
  5.3 0.1 add_select_fusion.2
  5.3 0.1 copy.22
  5.4 0.7 select_reduce_fusion.4.last
  6.1 0.7 select_reduce_fusion.5.keep
  6.7 0.1 iota_add_fusion.1
  6.8 0.7 add.191.final_row
  7.5 0.9 convert_reduce_fusion
  8.4 0.1 fusion
  8.5 0.8 select_reduce_fusion
  9.3 0.1 fusion.8
  9.4 0.7 select_reduce_fusion.6
  10.1 0.1 select_reduce_fusion.2
  10.2 0.6 fusion.3.b_row
  10.8 175.3 %shard_map.131 = (f32[1024,256]{1,0:T(8,128)}, bf16[64,128,256]{2,1,0:T(8,128)(2,1)}) custom-call(s32[8,56]{1,0:T(8,128)} %get-tuple-element.9.a_idx, s32[8,56]{1,0:T(8,128)} %fusion.3.b_row, f32[8,28]{1,0:T(8,128)} %select_reduce_fusion.5.keep, s32[8,8]{1,0:T(8,128)} %select_reduce_fusion.4.last, s32[1,64]{1,0:T(1,128)} %add.191.final_row, ...), custom_call_target="tpu_custom_call" | custom-call | tf_op jit(solution)/shard_map/pallas_call | solution.py:279
  186.1 2.3 %copy.25 = f32[1,1,1024,256]{3,2,1,0:T(8,128)} copy(f32[1,1,1024,256]{3,2,1,0:T(8,128)} %bitcast.22) | data formatting | bytes 2097152
  188.4 4.5 %copy.26 = bf16[1,8192,256]{2,1,0:T(8,128)(2,1)} copy(bf16[1,8192,256]{2,1,0:T(8,128)(2,1)} %bitcast.19) | data formatting | bytes 8388608
  (19 shorter events, 0.1 us)

commit v2 on v1

v2 whole, which is shorter than its diff:
```python
import functools

import jax
import jax.numpy as jnp
from jax import lax
from jax.experimental import pallas as pl
from jax.experimental.pallas import tpu as pltpu
from jax.sharding import PartitionSpec as P

MESH = pl.DeviceIdType.MESH
UNROLL = 4


def cuts(nb):
    return [2] * (nb // 2) + [1] * (nb % 2)


def pair_count(tiles, nb):
    pairs = (tiles + nb) // 2
    return -(-pairs // UNROLL) * UNROLL


def kernel(
    layers, streams, per_stream, beats, rows, tb, pairs,
    code, tpos, apos,
    act_ref, feed_ref, tile_ref, hist_ref, mix_ref, gain_ref, up_ref, down_ref,
    out_ref, all_ref, cur_ref,
    hist, tiles, land, stage, segs, sbuf,
    tile_of, block_of, keep_of, last_of, cur,
    local_sem, hist_sem, tile_sem, old_sem, new_sem, y_send, y_recv, sib_send, sib_recv, x_send, x_recv, r_send, r_recv,
):
    layer = lax.axis_index("layer")
    me = lax.axis_index("group")
    core = lax.rem(me, 2)
    sib = me + 1 - 2 * core
    cross = lax.rem(me + 2, streams)
    cross_sib = cross + 1 - 2 * core
    nb = rows // tb
    sizes = cuts(nb)
    chunks = len(sizes)
    starts = [sum(sizes[:k]) for k in range(chunks)]
    slots = streams * per_stream
    first_layer = layer == 0
    last_layer = layer == layers - 1

    old = pltpu.make_async_copy(hist_ref, hist.at[pl.ds(0, slots * nb)], hist_sem)
    old.start()
    load = pltpu.make_async_copy(tile_ref, tiles.at[pl.ds(0, tile_ref.shape[0])], tile_sem)
    load.start()
    tiles[tile_ref.shape[0]] = jnp.zeros((tb, tb), jnp.bfloat16)
    segs[pairs] = jnp.zeros((tb, hist.shape[2]), jnp.bfloat16)

    barrier = pltpu.get_barrier_semaphore()
    for peer in (sib, cross):
        pl.semaphore_signal(barrier, inc=1, device_id={"group": peer}, device_id_type=MESH)

    @pl.when(layer > 0)
    def _():
        pl.semaphore_signal(barrier, inc=1, device_id={"layer": layer - 1}, device_id_type=MESH)

    @pl.when(layer < layers - 1)
    def _():
        pl.semaphore_signal(barrier, inc=1, device_id={"layer": layer + 1}, device_id_type=MESH)

    inner = (layer > 0).astype(jnp.int32) + (layer < layers - 1).astype(jnp.int32)
    pl.semaphore_wait(barrier, 2 + inner)

    def piece(k):
        return pl.ds(starts[k] * tb, sizes[k] * tb)

    def y_copy(b, k):
        return pltpu.make_async_remote_copy(
            src_ref=sbuf.at[piece(k)],
            dst_ref=land.at[b, me, piece(k)],
            send_sem=y_send.at[k],
            recv_sem=y_recv.at[b, k],
            device_id={"layer": layer + 1},
            device_id_type=MESH,
        )

    def group_copy(b, k, stream, send, recv, to):
        return pltpu.make_async_remote_copy(
            src_ref=land.at[b, stream, piece(k)],
            dst_ref=land.at[b, stream, piece(k)],
            send_sem=send.at[k],
            recv_sem=recv.at[b, k],
            device_id={"group": to},
            device_id_type=MESH,
        )

    def keep_rows(b, stream, k):
        at = (slots + b * streams + stream) * nb
        for u in range(starts[k], starts[k] + sizes[k]):
            hist[at + u] = land[b, stream, pl.ds(u * tb, tb), :]

    def new_out(b):
        at = pl.ds((slots + b * streams) * nb, streams * nb)
        return pltpu.make_async_copy(hist.at[at], all_ref.at[at], new_sem.at[b])

    old_at = pl.ds(0, slots * nb)
    old_out = pltpu.make_async_copy(hist.at[old_at], all_ref.at[old_at], old_sem)
    blocks = slots * nb
    wide = 2 * nb

    def decode():
        for j in range(per_stream):
            for k in range(nb):
                last_of[j, k] = pairs

            def one(q, carry):
                for u in range(2):
                    i = 2 * q + u
                    x = code[j, i]
                    rest = lax.div(x, 2 * wide)
                    tile_of[j, i] = lax.div(rest, blocks)
                    block_of[j, i] = lax.rem(rest, blocks)
                x = code[j, 2 * q]
                keep_of[j, q] = 1 - lax.rem(x, 2)
                to = lax.rem(lax.div(x, 2), wide)
                for k in range(nb):
                    last_of[j, k] = jnp.where(to == k, q, last_of[j, k])
                return carry

            lax.fori_loop(0, pairs, one, 0)

    for g in range(slots):
        cur[g] = g

    def slot_of(b, c):
        before = tpos[jnp.maximum(layer - b, 0), c]
        after = apos[c, jnp.maximum(b - 1 - layer, 0)]
        return jnp.where(layer >= b, before, after)

    def beat(b, carry):
        source = jnp.logical_or(b == 0, first_layer)

        @pl.when(b == 0)
        def _():
            c = pltpu.make_async_copy(act_ref, stage, local_sem)
            c.start()
            c.wait()

        @pl.when(jnp.logical_and(b > 0, first_layer))
        def _():
            c = pltpu.make_async_copy(feed_ref.at[jnp.maximum(b - 1, 0)], stage, local_sem)
            c.start()
            c.wait()

        def cross_in(k):
            group_copy(b, k, cross, x_send, x_recv, cross).wait_recv()
            group_copy(b, k, cross, r_send, r_recv, sib).start()
            keep_rows(b, cross, k)

        def sib_in(k):
            group_copy(b, k, sib, sib_send, sib_recv, sib).wait_recv()
            keep_rows(b, sib, k)

        def far_in(k):
            group_copy(b, k, cross_sib, r_send, r_recv, sib).wait_recv()
            keep_rows(b, cross_sib, k)

        for k in range(chunks):
            @pl.when(source)
            def _():
                land[b, me, piece(k), :] = stage[piece(k), :].astype(jnp.bfloat16)

            @pl.when(jnp.logical_not(source))
            def _():
                y_copy(b, k).wait_recv()

            group_copy(b, k, me, x_send, x_recv, cross).start()
            group_copy(b, k, me, sib_send, sib_recv, sib).start()
            keep_rows(b, me, k)
            if k == min(1, chunks - 1):
                @pl.when(b == 0)
                def _():
                    decode()
            if k > 0:
                cross_in(k - 1)
                sib_in(k - 1)
            if k > 1:
                far_in(k - 2)
        sib_in(chunks - 1)
        if chunks > 1:
            far_in(chunks - 2)
        for c in range(streams):
            new = slot_of(b, c)
            for j in range(per_stream):
                g = c * per_stream + j
                cur[g] = jnp.where(new == j, slots + b * streams + c, cur[g])
        own = slot_of(b, me)
        cross_in(chunks - 1)
        far_in(chunks - 1)
        new_out(b).start()

        @pl.when(b == 0)
        def _():
            old.wait()
            load.wait()
            old_out.start()

        def one_pair(q, total):
            def half(h):
                i = 2 * q + h
                block = block_of[own, i]
                at = cur[lax.div(block, nb)] * nb + lax.rem(block, nb)
                return tiles[tile_of[own, i]], hist[at]

            t0, b0 = half(0)
            t1, b1 = half(1)
            product = jnp.dot(
                jnp.concatenate([t0, t1], axis=1),
                jnp.concatenate([b0, b1], axis=0),
                preferred_element_type=jnp.float32,
            )
            total = total * keep_of[own, q].astype(jnp.float32) + product
            segs[q] = total.astype(jnp.bfloat16)
            return total

        def pair_step(s, total):
            for u in range(UNROLL):
                total = one_pair(s * UNROLL + u, total)
            return total

        width = hist.shape[2]
        lax.fori_loop(0, pairs // UNROLL, pair_step, jnp.zeros((tb, width), jnp.float32))

        def rows_step(k):
            blocks = []
            for u in range(starts[k], starts[k] + sizes[k]):
                blocks.append(segs[last_of[own, u]])
            agg = jnp.concatenate(blocks, axis=0) if len(blocks) > 1 else blocks[0]
            act = land[b, me, piece(k), :].astype(jnp.float32)
            mixed = act + jnp.maximum(
                jnp.dot(agg, mix_ref[...], preferred_element_type=jnp.float32), 0.0
            )
            scale = lax.rsqrt(jnp.mean(mixed * mixed, axis=-1, keepdims=True) + 1e-06)
            normed = (mixed * scale * gain_ref[...]).astype(jnp.bfloat16)
            hidden = jax.nn.gelu(
                jnp.dot(normed, up_ref[...], preferred_element_type=jnp.float32)
            ).astype(jnp.bfloat16)
            return mixed + jnp.dot(hidden, down_ref[...], preferred_element_type=jnp.float32)

        sends = jnp.logical_and(b < beats - 1, layer < layers - 1)
        for k in range(chunks):
            @pl.when(jnp.logical_and(b > 0, layer < layers - 1))
            def _():
                y_copy(b, k).wait_send()

            res = rows_step(k)

            @pl.when(b == beats - 1)
            def _():
                out_ref[piece(k), :] = res

            @pl.when(sends)
            def _():
                sbuf[piece(k), :] = res.astype(jnp.bfloat16)
                y_copy(b + 1, k).start()

        for k in range(chunks):
            group_copy(b, k, me, x_send, x_recv, cross).wait_send()
            group_copy(b, k, me, sib_send, sib_recv, sib).wait_send()
            group_copy(b, k, cross, r_send, r_recv, sib).wait_send()
        return carry

    lax.fori_loop(0, beats, beat, 0)

    for g in range(slots):
        cur_ref[g] = cur[g]
    old_out.wait()

    def drain(b, carry):
        new_out(b).wait()
        return carry

    lax.fori_loop(0, beats, drain, 0)


def settle(slots, nb, cur, out_ref, all_ref, res_ref, hist_ref, mid, tmp, in_sem, out_sem):
    def load(g):
        at = pl.ds(cur[g] * nb, nb)
        return pltpu.make_async_copy(all_ref.at[at], mid.at[pl.ds(g * nb, nb)], in_sem.at[g])

    def save(g):
        at = pl.ds(g * nb, nb)
        return pltpu.make_async_copy(mid.at[at], hist_ref.at[at], out_sem.at[g])

    first = pltpu.make_async_copy(out_ref, tmp, in_sem.at[slots])
    second = pltpu.make_async_copy(tmp, res_ref, out_sem.at[slots])
    first.start()
    for g in range(slots):
        load(g).start()
    first.wait()
    second.start()
    for g in range(slots):
        load(g).wait()
        save(g).start()
    for g in range(slots):
        save(g).wait()
    second.wait()


def tables(read, write, nb, blocks):
    per_stream, tiles = read.shape
    pairs = pair_count(tiles, nb)
    i32 = jnp.int32
    js = jnp.arange(per_stream, dtype=i32)
    ks = jnp.arange(nb, dtype=i32)
    ts = jnp.arange(tiles, dtype=i32)
    count = jnp.sum((write[:, None, :] == ks[None, :, None]).astype(i32), axis=2)
    half = (count + 1) // 2
    start = jnp.sum(jnp.where(write[:, :, None] > ks, half[:, None, :], 0), axis=2)
    rank = jnp.sum(
        ((write[:, :, None] == write[:, None, :]) & (ts[None, None, :] < ts[None, :, None])).astype(i32),
        axis=2,
    )
    place = 2 * start + rank
    tile = js[:, None] * tiles + ts
    word = ((tile * blocks + read) * (2 * nb) + write) * 2 + (rank == 0).astype(i32)
    pad = ((per_stream * tiles * blocks) * (2 * nb) + nb) * 2
    qs = jnp.arange(2 * pairs, dtype=i32)
    at = place[:, None, :] == qs[None, :, None]
    return pad + jnp.sum(jnp.where(at, (word - pad)[:, None, :], 0), axis=2)


def solution(mesh):
    layers = mesh.shape["layer"]
    streams = mesh.shape["group"]

    def local(act, feed, tpos, apos, tiles, read, write, hist, mix, gain, up, down):
        rows, width = act.shape[2:]
        per_stream, n_tiles, tb = tiles.shape[:3]
        beats = feed.shape[1]
        nb = rows // tb
        slots = streams * per_stream
        pairs = pair_count(n_tiles, nb)
        chunks = len(cuts(nb))
        total = (slots + beats * streams) * nb
        smem = pl.BlockSpec(memory_space=pltpu.SMEM)
        vmem = pl.BlockSpec(memory_space=pltpu.VMEM)
        hbm = pl.BlockSpec(memory_space=pl.ANY)
        dma = pltpu.SemaphoreType.DMA
        out, everything, cur = pl.pallas_call(
            functools.partial(kernel, layers, streams, per_stream, beats, rows, tb, pairs),
            out_shape=(
                jax.ShapeDtypeStruct((rows, width), jnp.float32),
                jax.ShapeDtypeStruct((total, tb, width), jnp.bfloat16),
                jax.ShapeDtypeStruct((slots,), jnp.int32),
            ),
            in_specs=[smem] * 3 + [hbm, hbm, hbm, hbm, vmem, vmem, vmem, vmem],
            out_specs=(vmem, hbm, smem),
            scratch_shapes=[
                pltpu.VMEM((total, tb, width), jnp.bfloat16),
                pltpu.VMEM((per_stream * n_tiles + 1, tb, tb), jnp.bfloat16),
                pltpu.VMEM((beats, streams, rows, width), jnp.bfloat16),
                pltpu.VMEM((rows, width), jnp.float32),
                pltpu.VMEM((pairs + 1, tb, width), jnp.bfloat16),
                pltpu.VMEM((rows, width), jnp.bfloat16),
                pltpu.SMEM((per_stream, 2 * pairs), jnp.int32),
                pltpu.SMEM((per_stream, 2 * pairs), jnp.int32),
                pltpu.SMEM((per_stream, pairs), jnp.int32),
                pltpu.SMEM((per_stream, nb), jnp.int32),
                pltpu.SMEM((slots,), jnp.int32),
                dma,
                dma,
                dma,
                dma,
                dma((beats,)),
                dma((chunks,)),
                dma((beats, chunks)),
                dma((chunks,)),
                dma((beats, chunks)),
                dma((chunks,)),
                dma((beats, chunks)),
                dma((chunks,)),
                dma((beats, chunks)),
            ],
            compiler_params=pltpu.CompilerParams(
                collective_id=0, has_side_effects=True, vmem_limit_bytes=64000000
            ),
        )(
            tables(read, write, nb, slots * nb),
            tpos,
            apos,
            act[0, 0],
            feed[0],
            tiles.reshape(per_stream * n_tiles, tb, tb),
            hist[0].reshape(slots * nb, tb, width),
            mix[0],
            gain,
            up[0],
            down[0],
        )
        res, hist_new = pl.pallas_call(
            functools.partial(settle, slots, nb),
            out_shape=(
                jax.ShapeDtypeStruct((rows, width), jnp.float32),
                jax.ShapeDtypeStruct((slots * nb, tb, width), jnp.bfloat16),
            ),
            in_specs=[smem, hbm, hbm],
            out_specs=(hbm, hbm),
            scratch_shapes=[
                pltpu.VMEM((slots * nb, tb, width), jnp.bfloat16),
                pltpu.VMEM((rows, width), jnp.float32),
                dma((slots + 1,)),
                dma((slots + 1,)),
            ],
        )(cur, out, everything)
        return res[None, None], hist_new.reshape(1, slots * rows, width)

    return jax.shard_map(
        local,
        mesh=mesh,
        in_specs=(
            P("layer", "group", None, None),
            P("group", None, None, None),
            P(),
            P(),
            P("group", None, None, None),
            P("group", None),
            P("group", None),
            P("layer", None, None),
            P("layer", None, None),
            P("layer", None),
            P("layer", None, None),
            P("layer", None, None),
        ),
        out_specs=(P("layer", "group", None, None), P("layer", None, None)),
        check_vma=False,
    )
```

time: 193 us -> 186 us (0.964)
  local copies, waits for them, and re-layouts: 8.86 us -> 1.35 us
  Pallas kernels: 175 us -> 179 us
  other arithmetic: 7.93 us -> 4.01 us
    unnamed x2 -> x1, local copies, waits for them, and re-layouts: 6.73 us -> 1.35 us
    pallas_call x0 -> x1, Pallas kernels: none -> 4.9 us  [local(): pl.pallas_call(functools.partial(settle, slots, nb), out_shape=(jax.Shape...]
    reduce_sum x8 -> x3, other arithmetic: 4.61 us -> 1.69 us  [the longest x1 0.82 us: tables(): jnp.sum((write[:, None, :] == ks[None, :, None]).astype(i32), axis=2)]
where the time goes in v2:
time: 186 us; the launch traced here: 185 us
  Pallas kernels  179 us (96%)
  other arithmetic  4.01 us (2%)
    pallas_call x1, Pallas kernels, local(): pl.pallas_call(functools.partial(kernel, layers, streams, per_stream, bea...  174 us
    pallas_call x1, Pallas kernels, local(): pl.pallas_call(functools.partial(settle, slots, nb), out_shape=(jax.Shape...  4.9 us

profile of v2, /device:TPU:31, one launch (start us, length us, event | category | flops | bytes accessed | tf_op | source)
XLA Modules:
  0.0 185.4 jit_solution(9501764938757570466)
XLA Ops:
  0.6 0.8 convert_reduce_fusion.1
  1.5 0.8 select_reduce_fusion.1
  2.2 1.3 copy.15.tpos
  3.6 0.9 convert_reduce_fusion
  4.5 0.8 multiply_add_fusion
  5.3 0.1 select_reduce_fusion
  5.4 0.6 broadcast_add_fusion.code
  6.0 174.4 %shard_map.131 = (f32[1024,256]{1,0:T(8,128)}, bf16[320,128,256]{2,1,0:T(8,128)(2,1)}, s32[8]{0:T(128)}) custom-call(s32[2,56]{1,0:T(2,128)} %broadcast_add_fusion.code, s32[8,4]{1,0:T(8,128)} %copy.15.tpos, s32[4,8]{1,0:T(4,128)} %apos.1, f32[1024,256]{1,0:T(8,128)} %bitcast.12, f32[8,1024,256]{2,1,0:T(8,128)} %bitcast.9, bf16[96,128,128]{2,1,0:T(8,128)(2,1)} %bitcast.11, ...), custom_call_target="tpu_custom_call" | custom-call | tf_op jit(solution)/shard_map/pallas_call | solution.py:344
  180.4 4.9 %shard_map.132 = (f32[1024,256]{1,0:T(8,128)}, bf16[64,128,256]{2,1,0:T(8,128)(2,1)}) custom-call(s32[8]{0:T(128)} %get-tuple-element.7.cur, f32[1024,256]{1,0:T(8,128)} %get-tuple-element.8.out_ref, bf16[320,128,256]{2,1,0:T(8,128)(2,1)} %get-tuple-element.9.all_ref), custom_call_target="tpu_custom_call" | custom-call | tf_op jit(solution)/shard_map/pallas_call | solution.py:395
  (3 shorter events, 0.0 us)
